TPU v7x, 32 devices: a whole 2x2x4 slice. The times are simulated.
32 devices in a mesh: ctx: 8 (over z, y), grp: 4 (over x, core).
Axes of the slice: x: 2, y: 2, z: 4, core: 2. Of those that a mesh axis runs over, the one named last changes fastest.
Arguments:
- tokens: bfloat16 [4, 512, 8192], P('grp', 'ctx'), may hold values from -6 to 6
- queries: bfloat16 [4, 512, 4096], P('grp', 'ctx'), may hold values from -32 to 32
- key_value_weight: bfloat16 [8192, 1024], P('grp'), may hold values from -0.0625 to 0.0625
- adapter_down_weight: bfloat16 [8192, 128], P('grp'), may hold values from -0.0625 to 0.0625
- adapter_up_weight: bfloat16 [2, 64, 512], replicated, may hold values from -0.75 to 0.75
- tile_request_mask: int32 [4, 4, 4], P('grp'), may hold values 0 or 1
- lengths: int32 [4], P('grp'), may hold values from 128 to 512, as said below
- page_lookup_table: int32 [4, 128], P(None, 'ctx'), may hold values from 0 to 63, as said below
Outputs:
- attended: bfloat16 [4, 512, 4096], P('grp', 'ctx')
- decode_cache: bfloat16 [4, 128, 4, 1024], P('grp', 'ctx')
Inputs may be any that keep to these rules, and one draw needn't show every extreme that they name: `page_lookup_table`: pages of positions held by one index of ctx go to decode-cache rows of that same index. Every decode group receives exactly 16 pages into distinct slots from the pages of each index of ctx. From the pages of one rollout on one index of ctx, at most max(2, ceil(4)) go to one group, and exactly that many to some group. `lengths`: some rollout has all 512 positions live.
All inputs are finite; a program needn't handle non-finite values. No bound on the sum of `tile_request_mask` on one device may be relied on, other than what follows from the above.
Results may differ from a plain program's by a relative error of at most 0.028.
Values may be sent and summed in bfloat16 or wider, within the bound.
A program may use at most 64 MiB of HBM per device.

v0:
```python
import jax
import jax.numpy as jnp
from jax import lax
from jax.sharding import PartitionSpec as P

HEAD_SIZE = 128
HQ = 32
KEY_VALUE_HEADS = 4
PAGE = 4
TILE = 128
THETA = 500000.0
ADAPTER_SCALE = 0.5


def rotate(key_rows, token_positions):
    half_split = HEAD_SIZE // 2
    freq = THETA ** (-(2.0 * jnp.arange(half_split, dtype=jnp.float32)) / HEAD_SIZE)
    angle = token_positions.astype(jnp.float32)[:, None] * freq[None, :]
    cosine = jnp.cos(angle)[:, None, :]
    sine = jnp.sin(angle)[:, None, :]
    first = key_rows[..., :half_split]
    second = key_rows[..., half_split:]
    return jnp.concatenate([first * cosine - second * sine, second * cosine + first * sine], -1)


def send_pages(own, page_lookup_table, groups):
    column_width = own.shape[1]
    ppd = own.shape[0] // PAGE
    most = max(2, -(-ppd // groups))
    me = lax.axis_index("grp")
    dest = page_lookup_table // ppd
    slot = page_lookup_table % ppd
    earlier = jnp.arange(ppd)[:, None] > jnp.arange(ppd)[None, :]
    same = dest[:, :, None] == dest[:, None, :]
    order = jnp.sum(same & earlier[None], axis=2)
    my_dest = lax.dynamic_index_in_dim(dest, me, 0, keepdims=False)
    my_order = lax.dynamic_index_in_dim(order, me, 0, keepdims=False)
    pick = (my_dest[None, None, :] == jnp.arange(groups)[:, None, None]) & (
        my_order[None, None, :] == jnp.arange(most)[None, :, None]
    )
    pages = own.reshape(ppd, PAGE * column_width)
    outgoing = jnp.einsum(
        "gck,kf->gcf", pick.astype(jnp.bfloat16), pages, preferred_element_type=jnp.float32
    ).astype(jnp.bfloat16)
    incoming = lax.all_to_all(outgoing, "grp", split_axis=0, concat_axis=0, tiled=True)
    place = (
        (dest[None, :, None, :] == me)
        & (order[None, :, None, :] == jnp.arange(most)[None, None, :, None])
        & (slot[None, :, None, :] == jnp.arange(ppd)[:, None, None, None])
    )
    place = jnp.any(place, axis=3).reshape(ppd, groups * most)
    cache = jnp.dot(
        place.astype(jnp.bfloat16),
        incoming.reshape(groups * most, PAGE * column_width),
        preferred_element_type=jnp.float32,
    )
    return cache.astype(jnp.bfloat16).reshape(1, ppd, PAGE, column_width)


def local(
    tokens,
    queries,
    key_value_weight,
    adapter_down_weight,
    adapter_up_weight,
    tile_request_mask,
    lengths,
    page_lookup_table,
):
    groups = lax.axis_size("grp")
    tok = tokens.shape[1]
    column_width = key_value_weight.shape[1]
    half_split = column_width // 2
    rank_count = adapter_up_weight.shape[1]
    group = HQ // KEY_VALUE_HEADS
    ctx_pos = lax.axis_index("ctx")
    token_positions = ctx_pos * tok + jnp.arange(tok, dtype=jnp.int32)
    mixed_output = lax.all_to_all(tokens[0], "grp", split_axis=1, concat_axis=0, tiled=True)
    summed_output = lax.psum_scatter(
        jnp.concatenate(
            [
                jnp.dot(mixed_output, key_value_weight, preferred_element_type=jnp.float32),
                jnp.dot(mixed_output, adapter_down_weight, preferred_element_type=jnp.float32),
            ],
            1,
        ).astype(jnp.bfloat16),
        "grp",
        scatter_dimension=0,
        tiled=True,
    ).astype(jnp.float32)
    low_rank_state = summed_output[:, column_width:].astype(jnp.bfloat16)
    key_rows = summed_output[:, :half_split] + ADAPTER_SCALE * jnp.dot(
        low_rank_state[:, :rank_count], adapter_up_weight[0], preferred_element_type=jnp.float32
    )
    value_rows = summed_output[:, half_split:column_width] + ADAPTER_SCALE * jnp.dot(
        low_rank_state[:, rank_count:], adapter_up_weight[1], preferred_element_type=jnp.float32
    )
    key_rows = rotate(key_rows.reshape(tok, KEY_VALUE_HEADS, HEAD_SIZE), token_positions).reshape(
        tok, half_split
    )
    own = jnp.concatenate([key_rows, value_rows], 1).astype(jnp.bfloat16)
    decode_cache = send_pages(own, page_lookup_table, groups)
    query_heads = queries[0].reshape(tok, KEY_VALUE_HEADS, group, HEAD_SIZE)
    scale = 1.0 / HEAD_SIZE**0.5
    tiles = tile_request_mask.shape[1]
    tile_ids = jnp.arange(tiles, dtype=jnp.int32)
    query_tile = token_positions // TILE
    query_onehot = (query_tile[:, None] == tile_ids[None, :]).astype(jnp.float32)
    live_rows = jnp.dot(query_onehot, tile_request_mask[0].astype(jnp.float32))
    length = lengths[0]
    initial = (
        jnp.full((KEY_VALUE_HEADS, group, tok, 1), -1e30, jnp.float32),
        jnp.zeros((KEY_VALUE_HEADS, group, tok, 1), jnp.float32),
        jnp.zeros((KEY_VALUE_HEADS, group, tok, HEAD_SIZE), jnp.float32),
    )
    state = initial
    piece = lax.all_gather(own, "ctx", axis=0, tiled=True)
    count = piece.shape[0]
    blk = 512
    blocks = piece.reshape(count // blk, blk, column_width)

    def inner(carry, item):
        offset, block = item
        peak, total, acc = carry
        kpos = offset * blk + jnp.arange(blk, dtype=jnp.int32)
        key_block = block[:, :half_split].reshape(blk, KEY_VALUE_HEADS, HEAD_SIZE)
        value_block = (
            block[:, half_split:].reshape(blk, KEY_VALUE_HEADS, HEAD_SIZE).astype(jnp.float32)
        )
        score = (
            jnp.einsum("qhgd,khd->hgqk", query_heads, key_block, preferred_element_type=jnp.float32)
            * scale
        )
        key_tile = kpos // TILE
        key_onehot = (key_tile[:, None] == tile_ids[None, :]).astype(jnp.float32)
        live = jnp.dot(live_rows, key_onehot.T) > 0.5
        live = live | (query_tile[:, None] == key_tile[None, :])
        allowed = (kpos[None, :] <= token_positions[:, None]) & (kpos[None, :] >= 0) & live & (
            kpos[None, :] < length
        ) | (kpos[None, :] == token_positions[:, None])
        masked = jnp.where(allowed, score, -1e30)
        new_peak = jnp.maximum(peak, jnp.max(masked, axis=-1, keepdims=True))
        expo = jnp.where(allowed, jnp.exp(masked - new_peak), 0.0)
        factor = jnp.exp(peak - new_peak)
        total = total * factor + jnp.sum(expo, axis=-1, keepdims=True)
        acc = acc * factor + jnp.einsum(
            "hgqk,khd->hgqd", expo, value_block, preferred_element_type=jnp.float32
        )
        return ((new_peak, total, acc), None)

    offsets = jnp.arange(count // blk, dtype=jnp.int32)
    state, _ = lax.scan(inner, state, (offsets, blocks))
    peak, total, acc = state
    out = acc / total
    out = jnp.transpose(out, (2, 0, 1, 3)).reshape(tok, HQ * HEAD_SIZE)
    out = jnp.where((token_positions < length)[:, None], out, 0.0)
    attended = out.astype(jnp.bfloat16)[None]
    return (attended, decode_cache)


def solution(mesh):
    in_specs = (
        P("grp", "ctx", None),
        P("grp", "ctx", None),
        P("grp", None),
        P("grp", None),
        P(),
        P("grp", None, None),
        P("grp"),
        P(None, "ctx"),
    )
    out_specs = (P("grp", "ctx", None), P("grp", "ctx", None, None))
    return jax.shard_map(local, mesh=mesh, in_specs=in_specs, out_specs=out_specs, check_vma=False)
```

profile of v0, /device:TPU:0, one launch (start us, length us, event | category | flops | bytes accessed | tf_op | source)
XLA Modules:
  0.0 115.5 jit_solution(12051520847819461086)
XLA Ops:
  7.2 0.0 copy-start
  7.2 1.9 %all_to_all.17 = bf16[64,4,2048]{2,1,0:T(4,128)(2,1)S(1)} reshape(bf16[1,64,8192]{2,1,0:T(8,128)(2,1)} %param.8) | data formatting | bytes 2097152 | tf_op jit(solution)/shard_map/all_to_all | solution.py:78
  9.1 1.5 %copy.31 = bf16[64,4,2048]{2,0,1:T(8,128)(2,1)} copy(bf16[64,4,2048]{2,1,0:T(4,128)(2,1)S(1)} %all_to_all.17) | data formatting | bytes 2097152 | tf_op jit(solution)/shard_map/all_to_all | solution.py:78
  10.6 4.2 %all-to-all-start = ((bf16[64,4,2048]{2,0,1:T(8,128)(2,1)}), bf16[64,4,2048]{2,0,1:T(8,128)(2,1)S(1)}, u32[]{:S(2)}, u32[]{:S(2)}) async-start(bf16[64,4,2048]{2,0,1:T(8,128)(2,1)} %copy.31), calls=%async_computation | async-start | bytes 2097152 | tf_op jit(solution)/shard_map/all_to_all | solution.py:78
  14.8 0.0 reduce-scatter.2.cloned.1.call-start
  14.9 14.4 %all-to-all-done = bf16[64,4,2048]{2,0,1:T(8,128)(2,1)S(1)} async-done(((bf16[64,4,2048]{2,0,1:T(8,128)(2,1)}), bf16[64,4,2048]{2,0,1:T(8,128)(2,1)S(1)}, u32[]{:S(2)}, u32[]{:S(2)}) %all-to-all-start) | async-done | bytes 1048608 | tf_op jit(solution)/shard_map/all_to_all | solution.py:78
  29.3 0.0 copy-done
  29.3 0.4 convolution_convert_fusion.2
  29.7 0.0 copy-start.3
  29.8 0.0 copy-start.2
  29.8 0.0 copy-start.1
  29.8 3.5 %convolution_convert_fusion.1 = bf16[256,1024]{1,0:T(8,128)(2,1)S(1)} fusion(bf16[256,2048]{1,0:T(8,128)(2,1)S(1)} %bitcast.71, bf16[2048,1024]{1,0:T(8,128)(2,1)} %param.10), kind=kOutput, calls=%fused_computation.15 | convolution fusion | flops 1074003968 | bytes 5767168 | tf_op jit(solution)/shard_map/dot_general | solution.py:82
  33.3 0.0 copy-start.4
  33.3 0.9 pad_maximum_fusion
  34.2 0.0 reduce-scatter.2.cloned.1.call-update
  34.2 0.0 all-gather.2.cloned.1.call-start
  34.9 0.0 copy-done.3
  35.0 0.2 convert_reduce_fusion
  35.2 0.2 multiply_cosine_fusion
  35.4 22.0 %reduce-scatter.2.cloned.1.call-done = bf16[64,1152]{1,0:T(8,128)(2,1)} async-done(((bf16[256,1152]{1,0:T(8,128)(2,1)}), bf16[64,1152]{1,0:T(8,128)(2,1)}) %reduce-scatter.2.cloned.1.call-update) | async-done | bytes 147472 | tf_op jit(solution)/shard_map/reduce_scatter | solution.py:79
  57.4 0.9 convert_element_type.53
  58.4 0.0 copy-done.2
  58.4 0.9 fusion.12
  59.3 0.2 multiply_subtract_fusion
  59.5 0.1 pad_maximum_fusion.1
  59.6 0.9 fusion.11
  60.5 0.7 maximum_convert_fusion
  61.2 0.0 all-gather.2.cloned.1.call-update
  61.2 0.0 copy-done.1
  61.2 0.1 copy.45
  61.4 0.4 and_reduce_fusion
  61.8 0.4 fusion.16
  62.2 1.0 reshape.298
  63.2 0.8 convolution_convert_fusion
  64.1 3.3 %all-to-all-start.1 = ((bf16[4,4,4096]{2,1,0:T(4,128)(2,1)}), bf16[4,4,4096]{2,1,0:T(4,128)(2,1)S(1)}, u32[]{:S(2)}, u32[]{:S(2)}) async-start(bf16[4,4,4096]{2,1,0:T(4,128)(2,1)} %convolution_convert_fusion), calls=%async_computation.2 | async-start | bytes 262144 | tf_op jit(solution)/shard_map/all_to_all | solution.py:45
  67.4 4.6 %all-to-all-done.1 = bf16[4,4,4096]{2,1,0:T(4,128)(2,1)S(1)} async-done(((bf16[4,4,4096]{2,1,0:T(4,128)(2,1)}), bf16[4,4,4096]{2,1,0:T(4,128)(2,1)S(1)}, u32[]{:S(2)}, u32[]{:S(2)}) %all-to-all-start.1) | async-done | bytes 131104 | tf_op jit(solution)/shard_map/all_to_all | solution.py:45
  72.0 0.2 fusion
  72.2 0.7 reshape.295
  73.0 28.6 %all-gather.2.cloned.1.call-done = bf16[512,1024]{1,0:T(8,128)(2,1)} async-done(((bf16[64,1024]{1,0:T(8,128)(2,1)}), bf16[512,1024]{1,0:T(8,128)(2,1)}) %all-gather.2.cloned.1.call-update) | async-done | bytes 1048592 | tf_op jit(solution)/shard_map/all_gather | solution.py:117
  101.6 1.3 %fusion.49 = (bf16[512,512]{1,0:T(8,128)(2,1)S(1)}, bf16[512,512]{1,0:T(8,128)(2,1)S(1)}) fusion(bf16[512,1024]{1,0:T(8,128)(2,1)} %all-gather.2.cloned.1.call-done), kind=kLoop, calls=%fused_computation.99 | loop fusion | bytes 2097152 | tf_op jit(solution)/shard_map/while/body/eval_jaxpr/slice | solution.py:128
  102.9 0.1 reshape.293
  103.0 0.1 reshape.292
  103.1 1.0 fusion.1
  104.2 1.3 %fusion.2 = f32[4,8,64]{2,1,0:T(8,128)S(1)} fusion(f32[4,512,64,8]{1,2,3,0:T(8,128)S(1)} %get-tuple-element.46, f32[4,8,64]{2,1,0:T(8,128)S(1)} %get-tuple-element.31, pred[64,512]{1,0:T(8,128)(4,1)S(1)} %fusion.16), kind=kLoop, calls=%fused_computation.6 | loop fusion | flops 5240832 | bytes 4243456 | tf_op jit(solution)/shard_map/while/body/eval_jaxpr/reduce_sum | solution.py:145
  105.5 1.6 %fusion.19 = bf16[64,4,8,128]{3,0,2,1:T(8,128)(2,1)S(1)} fusion(f32[4,512,64,8]{1,2,3,0:T(8,128)S(1)} %get-tuple-element.46, f32[4,8,64]{2,1,0:T(8,128)S(1)} %get-tuple-element.31, pred[64,512]{1,0:T(8,128)(4,1)S(1)} %fusion.16, bf16[512,4,128,1]{2,1,0,3:T(4,128)(2,1)S(1)} %bitcast.74, f32[64,4,8]{0,2,1:T(8,128)S(1)} %bitcast_add_fusion, ...), kind=kOutput, calls=%fused_computation.28 | convolution fusion | flops 273416192 | bytes 5300224 | tf_op jit(solution)/shard_map/while/body/eval_jaxpr/hgqk,khd->hgqd/dot_general | solution.py:146
  107.1 0.3 copy.36
  107.5 0.2 reshape.294
  107.7 1.0 select_convert_fusion
  (19 shorter events, 0.2 us)
Async XLA Ops:
  7.2 22.1 %copy-start = (bf16[2048,128]{1,0:T(8,128)(2,1)S(1)}, bf16[2048,128]{1,0:T(8,128)(2,1)}, u32[]{:S(2)}) copy-start(bf16[2048,128]{1,0:T(8,128)(2,1)} %param.11) | copy-start | bytes 1572868
  10.6 18.7 %all-to-all-start = ((bf16[64,4,2048]{2,0,1:T(8,128)(2,1)}), bf16[64,4,2048]{2,0,1:T(8,128)(2,1)S(1)}, u32[]{:S(2)}, u32[]{:S(2)}) async-start(bf16[64,4,2048]{2,0,1:T(8,128)(2,1)} %copy.31), calls=%async_computation | async-start | bytes 2097152 | tf_op jit(solution)/shard_map/all_to_all | solution.py:78
  14.8 42.6 %reduce-scatter.2.cloned.1.call-start = ((), (), s32[]{:S(2)}) async-start(), calls=%async_computation.3 | async-start | bytes 737280 | tf_op jit(solution)/shard_map/reduce_scatter | solution.py:79
  29.7 5.2 %copy-start.3 = (s32[4,16]{1,0:T(4,128)S(1)}, s32[4,16]{1,0:T(4,128)}, u32[]{:S(2)}) copy-start(s32[4,16]{1,0:T(4,128)} %param.15) | copy-start | bytes 772
  29.8 28.6 %copy-start.2 = (bf16[2,64,512]{2,1,0:T(8,128)(2,1)S(1)}, bf16[2,64,512]{2,1,0:T(8,128)(2,1)}, u32[]{:S(2)}) copy-start(bf16[2,64,512]{2,1,0:T(8,128)(2,1)} %param.12) | copy-start | bytes 393220
  29.8 31.5 %copy-start.1 = (bf16[1,64,4096]{2,1,0:T(8,128)(2,1)S(1)}, bf16[1,64,4096]{2,1,0:T(8,128)(2,1)}, u32[]{:S(2)}) copy-start(bf16[1,64,4096]{2,1,0:T(8,128)(2,1)} %param.9) | copy-start | bytes 1572868
  33.3 28.5 %copy-start.4 = (s32[1,4,4]{2,1,0:T(4,128)S(1)}, s32[1,4,4]{2,1,0:T(4,128)}, u32[]{:S(2)}) copy-start(s32[1,4,4]{2,1,0:T(4,128)} %param.13) | copy-start | bytes 196
  34.2 67.4 %all-gather.2.cloned.1.call-start = ((), (), s32[]{:S(2)}) async-start(), calls=%async_computation.4 | async-start | bytes 1179648 | tf_op jit(solution)/shard_map/all_gather | solution.py:117
  64.1 7.9 %all-to-all-start.1 = ((bf16[4,4,4096]{2,1,0:T(4,128)(2,1)}), bf16[4,4,4096]{2,1,0:T(4,128)(2,1)S(1)}, u32[]{:S(2)}, u32[]{:S(2)}) async-start(bf16[4,4,4096]{2,1,0:T(4,128)(2,1)} %convolution_convert_fusion), calls=%async_computation.2 | async-start | bytes 262144 | tf_op jit(solution)/shard_map/all_to_all | solution.py:45
Sparse Core Ops, SparseCore 0:
  34.3 23.0 reduce-scatter.1
  61.3 40.2 all-gather.1
where the time goes:
time: 116 us; the launch traced here: 115 us
  waiting for transfers between devices  69.7 us (60%)
  between operations  15 us (13%)
  matrix products  9.79 us (8%)
  starting transfers between devices  7.58 us (7%)
  local copies, waits for them, and re-layouts  7.46 us (6%)
  other arithmetic  5.95 us (5%)
    all_gather x1, waiting for transfers between devices, local(): piece = lax.all_gather(own, 'ctx', axis=0, tiled=True)  28.6 us
    reduce_scatter x1, waiting for transfers between devices, local(): lax.psum_scatter(jnp.concatenate([jnp.dot(mixed_output, key_value_weight,...  22 us
    all_to_all x1, waiting for transfers between devices, local(): lax.all_to_all(tokens[0], 'grp', split_axis=1, concat_axis=0, tiled=True)  14.4 us
    all_to_all x1, waiting for transfers between devices, send_pages(): lax.all_to_all(outgoing, 'grp', split_axis=0, concat_axis=0, tiled=True)  4.58 us
    all_to_all x1, starting transfers between devices, local(): lax.all_to_all(tokens[0], 'grp', split_axis=1, concat_axis=0, tiled=True)  4.21 us
    dot_general x1, matrix products, local(): jnp.dot(mixed_output, key_value_weight, preferred_element_type=jnp.float32)  3.5 us
    all_to_all x2, local copies, waits for them, and re-layouts, local(): lax.all_to_all(tokens[0], 'grp', split_axis=1, concat_axis=0, tiled=True)  3.45 us
    all_to_all x1, starting transfers between devices, send_pages(): lax.all_to_all(outgoing, 'grp', split_axis=0, concat_axis=0, tiled=True)  3.33 us
  transfers between devices with their start and end apart: 4, of which 4 were waited for; matrix products, arithmetic and copies ran while one was open for 4% of the time, Pallas kernels for 0%

commit v1 on v0

--- a/solution.py
+++ b/solution.py
@@ -1,3 +1,4 @@
+import functools
 import jax
 import jax.numpy as jnp
 from jax import lax
@@ -10,6 +11,31 @@
 TILE = 128
 THETA = 500000.0
 ADAPTER_SCALE = 0.5
+
+
+def axis_part_return_all(unit, row_dim):
+    kept_arr = list(unit.shape[1:])
+    kept_arr[row_dim] *= unit.shape[0]
+    return jnp.moveaxis(unit, 0, row_dim).reshape(kept_arr)
+
+
+def records_perform(piece_in, axis_id, d0):
+    parts_n = lax.axis_size(axis_id)
+    in_order = [(ix, (ix + 1) % parts_n) for ix in range(parts_n)]
+    chunks = [(p, s) for s, p in in_order]
+    y2, formed = ([], [])
+    for dd in range(parts_n - 1):
+        if dd % 2 == 0:
+            y2.append(lax.ppermute(y2[-1] if y2 else piece_in, axis_id, in_order))
+        else:
+            formed.append(lax.ppermute(formed[-1] if formed else piece_in, axis_id, chunks))
+    b_now = jnp.stack([*y2[::-1], piece_in, *formed], axis=0)
+    x_new = lax.axis_index(axis_id) - len(y2)
+    b_now = b_now[(jnp.arange(parts_n) - x_new) % parts_n]
+    return axis_part_return_all(b_now, d0)
+
+
+plate_prepare = functools.partial(records_perform, axis_id="ctx", d0=0)
 
 
 def rotate(key_rows, token_positions):
@@ -114,7 +140,7 @@
         jnp.zeros((KEY_VALUE_HEADS, group, tok, HEAD_SIZE), jnp.float32),
     )
     state = initial
-    piece = lax.all_gather(own, "ctx", axis=0, tiled=True)
+    piece = plate_prepare(own)
     count = piece.shape[0]
     blk = 512
     blocks = piece.reshape(count // blk, blk, column_width)

time: 116 us -> 110 us (0.948)
  waiting for transfers between devices: 69.7 us -> 49.7 us
  starting transfers between devices: 7.58 us -> 23.9 us
  local copies, waits for them, and re-layouts: 7.46 us -> 6.27 us
    all_gather x1 -> x0, waiting for transfers between devices: 28.6 us -> none  [local(): piece = lax.all_gather(own, 'ctx', axis=0, tiled=True)]
    ppermute x0 -> x7, starting transfers between devices: none -> 16.4 us  [the longest x3 14.8 us: records_perform(): lax.ppermute(formed[-1] if formed else piece_in, axis_id, chunks)]
    ppermute x0 -> x7, waiting for transfers between devices: none -> 13.6 us  [the longest x4 8.84 us: records_perform(): y2.append(lax.ppermute(y2[-1] if y2 else piece_in, axis_id, in_order))]
    all_to_all x1, waiting for transfers between devices: 4.58 us -> 0.01 us  [send_pages(): lax.all_to_all(outgoing, 'grp', split_axis=0, concat_axis=0, tiled=True)]
    slice x1, local copies, waits for them, and re-layouts: 1.27 us -> 0.08 us  [inner(): key_block = block[:, :half_split].reshape(blk, KEY_VALUE_HEADS, HEAD_SIZE)]
  transfers between devices with their start and end apart: 4 -> 10, of which waited for: 4 -> 6; matrix products, arithmetic and copies ran while one was open for 4% -> 3% of each run, Pallas kernels for 0% -> 0%
where the time goes in v1:
time: 110 us
  waiting for transfers between devices  49.7 us (45%)
  starting transfers between devices  23.9 us (22%)
  between operations  15.1 us (14%)
  matrix products  9.72 us (9%)
  local copies, waits for them, and re-layouts  6.27 us (6%)
  other arithmetic  5.33 us (5%)
    reduce_scatter x1, waiting for transfers between devices, local(): lax.psum_scatter(jnp.concatenate([jnp.dot(mixed_output, key_value_weight,...  22.5 us
    ppermute x3, starting transfers between devices, records_perform(): lax.ppermute(formed[-1] if formed else piece_in, axis_id, chunks)  14.8 us
    all_to_all x1, waiting for transfers between devices, local(): lax.all_to_all(tokens[0], 'grp', split_axis=1, concat_axis=0, tiled=True)  13.5 us
    ppermute x4, waiting for transfers between devices, records_perform(): y2.append(lax.ppermute(y2[-1] if y2 else piece_in, axis_id, in_order))  8.84 us
    ppermute x3, waiting for transfers between devices, records_perform(): lax.ppermute(formed[-1] if formed else piece_in, axis_id, chunks)  4.77 us
    all_to_all x1, starting transfers between devices, local(): lax.all_to_all(tokens[0], 'grp', split_axis=1, concat_axis=0, tiled=True)  4.21 us
    dot_general x1, matrix products, local(): jnp.dot(mixed_output, key_value_weight, preferred_element_type=jnp.float32)  3.47 us
    all_to_all x2, local copies, waits for them, and re-layouts, local(): lax.all_to_all(tokens[0], 'grp', split_axis=1, concat_axis=0, tiled=True)  3.46 us
  transfers between devices with their start and end apart: 10, of which 6 were waited for; matrix products, arithmetic and copies ran while one was open for 3% of the time, Pallas kernels for 0%

profile of v1, /device:TPU:0, one launch (start us, length us, event | category | flops | bytes accessed | tf_op | source)
XLA Modules:
  0.0 109.9 jit_solution(952594658373295689)
XLA Ops:
  7.2 0.0 copy-start
  7.2 1.9 %all_to_all.17 = bf16[64,4,2048]{2,1,0:T(4,128)(2,1)S(1)} reshape(bf16[1,64,8192]{2,1,0:T(8,128)(2,1)} %param.8) | data formatting | bytes 2097152 | tf_op jit(solution)/shard_map/all_to_all | solution.py:104
  9.1 1.6 %copy.35 = bf16[64,4,2048]{2,0,1:T(8,128)(2,1)} copy(bf16[64,4,2048]{2,1,0:T(4,128)(2,1)S(1)} %all_to_all.17) | data formatting | bytes 2097152 | tf_op jit(solution)/shard_map/all_to_all | solution.py:104
  10.7 4.2 %all-to-all-start = ((bf16[64,4,2048]{2,0,1:T(8,128)(2,1)}), bf16[64,4,2048]{2,0,1:T(8,128)(2,1)S(1)}, u32[]{:S(2)}, u32[]{:S(2)}) async-start(bf16[64,4,2048]{2,0,1:T(8,128)(2,1)} %copy.35), calls=%async_computation | async-start | bytes 2097152 | tf_op jit(solution)/shard_map/all_to_all | solution.py:104
  15.6 0.2 convert_reduce_fusion
  15.9 13.5 %all-to-all-done = bf16[64,4,2048]{2,0,1:T(8,128)(2,1)S(1)} async-done(((bf16[64,4,2048]{2,0,1:T(8,128)(2,1)}), bf16[64,4,2048]{2,0,1:T(8,128)(2,1)S(1)}, u32[]{:S(2)}, u32[]{:S(2)}) %all-to-all-start) | async-done | bytes 1048608 | tf_op jit(solution)/shard_map/all_to_all | solution.py:104
  29.3 0.4 convolution_convert_fusion.2
  29.8 0.0 copy-start.4
  29.8 0.0 copy-start.2
  29.8 3.5 %convolution_convert_fusion.1 = bf16[256,1024]{1,0:T(8,128)(2,1)S(1)} fusion(bf16[256,2048]{1,0:T(8,128)(2,1)S(1)} %bitcast.102, bf16[2048,1024]{1,0:T(8,128)(2,1)} %param.10), kind=kOutput, calls=%fused_computation.16 | convolution fusion | flops 1074003968 | bytes 5767168 | tf_op jit(solution)/shard_map/dot_general | solution.py:108
  33.3 0.0 copy-start.1
  33.3 0.9 pad_maximum_fusion
  34.1 0.0 reduce-scatter.2.cloned.1.call-update
  34.2 0.4 fusion.16
  34.7 0.2 multiply_cosine_fusion
  34.9 22.5 %reduce-scatter.2.cloned.1.call-done = bf16[64,1152]{1,0:T(8,128)(2,1)} async-done(((bf16[256,1152]{1,0:T(8,128)(2,1)}), bf16[64,1152]{1,0:T(8,128)(2,1)}) %reduce-scatter.2.cloned.1.call-update) | async-done | bytes 147472 | tf_op jit(solution)/shard_map/reduce_scatter | solution.py:105
  57.4 0.9 convert_element_type.60
  58.4 0.9 fusion.12
  59.3 0.2 multiply_subtract_fusion
  59.5 0.1 pad_maximum_fusion.1
  59.6 0.9 fusion.11
  60.6 1.5 %collective-permute-start = (bf16[64,1024]{1,0:T(8,128)(2,1)S(1)}, bf16[64,1024]{1,0:T(8,128)(2,1)S(1)}, u32[]{:S(2)}, u32[]{:S(2)}) collective-permute-start(bf16[64,1024]{1,0:T(8,128)(2,1)S(1)} %maximum_convert_fusion), channel_id=1, source_target_pairs={{0,4},{4,8},{8,12},{12,16},{16,20},{20,24},{24,28},{28,0},{1,5},{5... | collective-permute-start | bytes 393224 | tf_op jit(solution)/shard_map/ppermute | solution.py:29
  62.1 6.4 %collective-permute-done = bf16[64,1024]{1,0:T(8,128)(2,1)S(1)} collective-permute-done((bf16[64,1024]{1,0:T(8,128)(2,1)S(1)}, bf16[64,1024]{1,0:T(8,128)(2,1)S(1)}, u32[]{:S(2)}, u32[]{:S(2)}) %collective-permute-start) | collective-permute-done | bytes 131104 | tf_op jit(solution)/shard_map/ppermute | solution.py:29
  68.5 0.0 collective-permute-start.1
  68.6 0.1 copy.53
  68.7 0.4 and_reduce_fusion
  69.0 0.1 reshape.385
  69.1 4.8 %collective-permute-start.4 = (bf16[64,1024]{1,0:T(8,128)(2,1)S(1)}, bf16[64,1024]{1,0:T(8,128)(2,1)S(1)}, u32[]{:S(2)}, u32[]{:S(2)}) collective-permute-start(bf16[64,1024]{1,0:T(8,128)(2,1)S(1)} %maximum_convert_fusion), channel_id=1, source_target_pairs={{4,0},{8,4},{12,8},{16,12},{20,16},{24,20},{28,24},{0,28},{5,1},{9... | collective-permute-start | bytes 393224 | tf_op jit(solution)/shard_map/ppermute | solution.py:31
  73.9 2.4 %collective-permute-done.1 = bf16[64,1024]{1,0:T(8,128)(2,1)S(1)} collective-permute-done((bf16[64,1024]{1,0:T(8,128)(2,1)S(1)}, bf16[64,1024]{1,0:T(8,128)(2,1)S(1)}, u32[]{:S(2)}, u32[]{:S(2)}) %collective-permute-start.1) | collective-permute-done | bytes 131104 | tf_op jit(solution)/shard_map/ppermute | solution.py:29
  76.3 0.0 collective-permute-start.2
  76.3 0.8 convolution_convert_fusion
  77.1 3.3 %all-to-all-start.1 = ((bf16[4,4,4096]{2,1,0:T(4,128)(2,1)}), bf16[4,4,4096]{2,1,0:T(4,128)(2,1)S(1)}, u32[]{:S(2)}, u32[]{:S(2)}) async-start(bf16[4,4,4096]{2,1,0:T(4,128)(2,1)} %convolution_convert_fusion), calls=%async_computation.2 | async-start | bytes 262144 | tf_op jit(solution)/shard_map/all_to_all | solution.py:71
  80.5 4.8 %collective-permute-start.5 = (bf16[64,1024]{1,0:T(8,128)(2,1)S(1)}, bf16[64,1024]{1,0:T(8,128)(2,1)S(1)}, u32[]{:S(2)}, u32[]{:S(2)}) collective-permute-start(bf16[64,1024]{1,0:T(8,128)(2,1)S(1)} %collective-permute-done.4), channel_id=1, source_target_pairs={{4,0},{8,4},{12,8},{16,12},{20,16},{24,20},{28,24},{0,28},{5,1},{9... | collective-permute-start | bytes 393224 | tf_op jit(solution)/shard_map/ppermute | solution.py:31
  85.3 0.2 fusion
  85.6 0.7 reshape.374
  86.3 2.4 %collective-permute-done.5 = bf16[64,1024]{1,0:T(8,128)(2,1)S(1)} collective-permute-done((bf16[64,1024]{1,0:T(8,128)(2,1)S(1)}, bf16[64,1024]{1,0:T(8,128)(2,1)S(1)}, u32[]{:S(2)}, u32[]{:S(2)}) %collective-permute-start.5) | collective-permute-done | bytes 131104 | tf_op jit(solution)/shard_map/ppermute | solution.py:31
  88.7 5.3 %collective-permute-start.6 = (bf16[64,1024]{1,0:T(8,128)(2,1)S(1)}, bf16[64,1024]{1,0:T(8,128)(2,1)S(1)}, u32[]{:S(2)}, u32[]{:S(2)}) collective-permute-start(bf16[64,1024]{1,0:T(8,128)(2,1)S(1)} %collective-permute-done.5), channel_id=1, source_target_pairs={{4,0},{8,4},{12,8},{16,12},{20,16},{24,20},{28,24},{0,28},{5,1},{9... | collective-permute-start | bytes 393224 | tf_op jit(solution)/shard_map/ppermute | solution.py:31
  94.1 2.4 %collective-permute-done.6 = bf16[64,1024]{1,0:T(8,128)(2,1)S(1)} collective-permute-done((bf16[64,1024]{1,0:T(8,128)(2,1)S(1)}, bf16[64,1024]{1,0:T(8,128)(2,1)S(1)}, u32[]{:S(2)}, u32[]{:S(2)}) %collective-permute-start.6) | collective-permute-done | bytes 131104 | tf_op jit(solution)/shard_map/ppermute | solution.py:31
  96.5 0.6 gather_fusion
  97.1 0.1 fusion.49
  97.2 0.2 copy.50
  97.4 0.2 copy.51
  97.6 0.9 fusion.1
  98.6 1.3 %fusion.2 = f32[4,8,64]{2,1,0:T(8,128)S(1)} fusion(f32[4,512,64,8]{1,2,3,0:T(8,128)S(1)} %get-tuple-element.46, f32[4,8,64]{2,1,0:T(8,128)S(1)} %get-tuple-element.31, pred[64,512]{1,0:T(8,128)(4,1)S(1)} %fusion.16), kind=kLoop, calls=%fused_computation.7 | loop fusion | flops 5240832 | bytes 4243456 | tf_op jit(solution)/shard_map/while/body/eval_jaxpr/reduce_sum | solution.py:171
  100.0 1.6 %fusion.19 = bf16[64,4,8,128]{3,0,2,1:T(8,128)(2,1)S(1)} fusion(bf16[512,4,128,1]{0,2,3,1:T(8,128)(2,1)S(1)} %bitcast.108, f32[4,512,64,8]{1,2,3,0:T(8,128)S(1)} %get-tuple-element.46, f32[4,8,64]{2,1,0:T(8,128)S(1)} %get-tuple-element.31, pred[64,512]{1,0:T(8,128)(4,1)S(1)} %fusion.16, f32[64,4,8]{0,2,1:T(8,128)S(1)} %bitcast_add_fusion, ...), kind=kOutput, calls=%fused_computation.29 | convolution fusion | flops 273416192 | bytes 5300224 | tf_op jit(solution)/shard_map/while/body/eval_jaxpr/hgqk,khd->hgqd/dot_general | solution.py:172
  101.6 0.3 copy.42
  101.9 0.2 reshape.373
  102.2 1.0 select_convert_fusion
  (42 shorter events, 0.4 us)
Async XLA Ops:
  7.2 22.2 %copy-start = (bf16[2048,128]{1,0:T(8,128)(2,1)S(1)}, bf16[2048,128]{1,0:T(8,128)(2,1)}, u32[]{:S(2)}) copy-start(bf16[2048,128]{1,0:T(8,128)(2,1)} %param.11) | copy-start | bytes 1572868
  7.2 8.4 %copy-start.3 = (s32[4,16]{1,0:T(4,128)S(1)}, s32[4,16]{1,0:T(4,128)}, u32[]{:S(2)}) copy-start(s32[4,16]{1,0:T(4,128)} %param.15) | copy-start | bytes 772
  10.7 18.7 %all-to-all-start = ((bf16[64,4,2048]{2,0,1:T(8,128)(2,1)}), bf16[64,4,2048]{2,0,1:T(8,128)(2,1)S(1)}, u32[]{:S(2)}, u32[]{:S(2)}) async-start(bf16[64,4,2048]{2,0,1:T(8,128)(2,1)} %copy.35), calls=%async_computation | async-start | bytes 2097152 | tf_op jit(solution)/shard_map/all_to_all | solution.py:104
  14.9 42.6 %reduce-scatter.2.cloned.1.call-start = ((), (), s32[]{:S(2)}) async-start(), calls=%async_computation.3 | async-start | bytes 737280 | tf_op jit(solution)/shard_map/reduce_scatter | solution.py:105
  29.8 4.5 %copy-start.4 = (s32[1,4,4]{2,1,0:T(4,128)S(1)}, s32[1,4,4]{2,1,0:T(4,128)}, u32[]{:S(2)}) copy-start(s32[1,4,4]{2,1,0:T(4,128)} %param.13) | copy-start | bytes 196
  29.8 28.6 %copy-start.2 = (bf16[2,64,512]{2,1,0:T(8,128)(2,1)S(1)}, bf16[2,64,512]{2,1,0:T(8,128)(2,1)}, u32[]{:S(2)}) copy-start(bf16[2,64,512]{2,1,0:T(8,128)(2,1)} %param.12) | copy-start | bytes 393220
  33.3 35.3 %copy-start.1 = (bf16[1,64,4096]{2,1,0:T(8,128)(2,1)S(1)}, bf16[1,64,4096]{2,1,0:T(8,128)(2,1)}, u32[]{:S(2)}) copy-start(bf16[1,64,4096]{2,1,0:T(8,128)(2,1)} %param.9) | copy-start | bytes 1572868
  60.6 8.0 %collective-permute-start = (bf16[64,1024]{1,0:T(8,128)(2,1)S(1)}, bf16[64,1024]{1,0:T(8,128)(2,1)S(1)}, u32[]{:S(2)}, u32[]{:S(2)}) collective-permute-start(bf16[64,1024]{1,0:T(8,128)(2,1)S(1)} %maximum_convert_fusion), channel_id=1, source_target_pairs={{0,4},{4,8},{8,12},{12,16},{16,20},{20,24},{24,28},{28,0},{1,5},{5... | collective-permute-start | bytes 393224 | tf_op jit(solution)/shard_map/ppermute | solution.py:29
  68.5 7.8 %collective-permute-start.1 = (bf16[64,1024]{1,0:T(8,128)(2,1)S(1)}, bf16[64,1024]{1,0:T(8,128)(2,1)S(1)}, u32[]{:S(2)}, u32[]{:S(2)}) collective-permute-start(bf16[64,1024]{1,0:T(8,128)(2,1)S(1)} %collective-permute-done), channel_id=1, source_target_pairs={{0,4},{4,8},{8,12},{12,16},{16,20},{20,24},{24,28},{28,0},{1,5},{5... | collective-permute-start | bytes 393224 | tf_op jit(solution)/shard_map/ppermute | solution.py:29
  69.1 11.4 %collective-permute-start.4 = (bf16[64,1024]{1,0:T(8,128)(2,1)S(1)}, bf16[64,1024]{1,0:T(8,128)(2,1)S(1)}, u32[]{:S(2)}, u32[]{:S(2)}) collective-permute-start(bf16[64,1024]{1,0:T(8,128)(2,1)S(1)} %maximum_convert_fusion), channel_id=1, source_target_pairs={{4,0},{8,4},{12,8},{16,12},{20,16},{24,20},{28,24},{0,28},{5,1},{9... | collective-permute-start | bytes 393224 | tf_op jit(solution)/shard_map/ppermute | solution.py:31
  76.3 9.0 %collective-permute-start.2 = (bf16[64,1024]{1,0:T(8,128)(2,1)S(1)}, bf16[64,1024]{1,0:T(8,128)(2,1)S(1)}, u32[]{:S(2)}, u32[]{:S(2)}) collective-permute-start(bf16[64,1024]{1,0:T(8,128)(2,1)S(1)} %collective-permute-done.1), channel_id=1, source_target_pairs={{0,4},{4,8},{8,12},{12,16},{16,20},{20,24},{24,28},{28,0},{1,5},{5... | collective-permute-start | bytes 393224 | tf_op jit(solution)/shard_map/ppermute | solution.py:29
  77.1 8.2 %all-to-all-start.1 = ((bf16[4,4,4096]{2,1,0:T(4,128)(2,1)}), bf16[4,4,4096]{2,1,0:T(4,128)(2,1)S(1)}, u32[]{:S(2)}, u32[]{:S(2)}) async-start(bf16[4,4,4096]{2,1,0:T(4,128)(2,1)} %convolution_convert_fusion), calls=%async_computation.2 | async-start | bytes 262144 | tf_op jit(solution)/shard_map/all_to_all | solution.py:71
  80.5 8.1 %collective-permute-start.5 = (bf16[64,1024]{1,0:T(8,128)(2,1)S(1)}, bf16[64,1024]{1,0:T(8,128)(2,1)S(1)}, u32[]{:S(2)}, u32[]{:S(2)}) collective-permute-start(bf16[64,1024]{1,0:T(8,128)(2,1)S(1)} %collective-permute-done.4), channel_id=1, source_target_pairs={{4,0},{8,4},{12,8},{16,12},{20,16},{24,20},{28,24},{0,28},{5,1},{9... | collective-permute-start | bytes 393224 | tf_op jit(solution)/shard_map/ppermute | solution.py:31
  85.3 8.7 %collective-permute-start.3 = (bf16[64,1024]{1,0:T(8,128)(2,1)S(1)}, bf16[64,1024]{1,0:T(8,128)(2,1)S(1)}, u32[]{:S(2)}, u32[]{:S(2)}) collective-permute-start(bf16[64,1024]{1,0:T(8,128)(2,1)S(1)} %collective-permute-done.2), channel_id=1, source_target_pairs={{0,4},{4,8},{8,12},{12,16},{16,20},{20,24},{24,28},{28,0},{1,5},{5... | collective-permute-start | bytes 393224 | tf_op jit(solution)/shard_map/ppermute | solution.py:29
  88.7 7.8 %collective-permute-start.6 = (bf16[64,1024]{1,0:T(8,128)(2,1)S(1)}, bf16[64,1024]{1,0:T(8,128)(2,1)S(1)}, u32[]{:S(2)}, u32[]{:S(2)}) collective-permute-start(bf16[64,1024]{1,0:T(8,128)(2,1)S(1)} %collective-permute-done.5), channel_id=1, source_target_pairs={{4,0},{8,4},{12,8},{16,12},{20,16},{24,20},{28,24},{0,28},{5,1},{9... | collective-permute-start | bytes 393224 | tf_op jit(solution)/shard_map/ppermute | solution.py:31
Sparse Core Ops, SparseCore 0:
  34.3 23.1 reduce-scatter.1
